TPU v7x, 128 devices: a whole 4x4x4 slice. The times are simulated.
128 devices in a mesh: rows: 64 (over y, x, z), feat: 2 (over core).
Axes of the slice: x: 4, y: 4, z: 4, core: 2. Of those that a mesh axis runs over, the one named last changes fastest.
Arguments:
- blocks: bfloat16 [8192, 8, 128, 128], P('rows', 'feat'), may hold values from -0.1875 to 0.1875
- col_index: int32 [8192, 8], P('rows', 'feat'), may hold values from 0 to 8191, as said below
- row_counts: int32 [8192, 2], P('rows', 'feat'), may hold values from 1 to 4, as said below
- labels: int32 [8192, 128], P('rows'), may hold values 0 or 1
- row_weight: float32 [8192, 128], P('rows'), may hold values from 0.3 to 9
- feature_scale: float32 [8192, 128], P('feat'), may hold values from 0.3 to 3
Outputs:
- solution: float32 [8192, 128], P('feat')
- last_resid: float32 [8192, 128], P('rows')
Inputs may be any that keep to these rules, and one draw needn't show every extreme that they name: `col_index`: a block in slot j of a row block names a feature block of half j // 4, that is from (j // 4) * 4096 to (j // 4 + 1) * 4096 - 1. `row_counts`: some row block of every index of rows has 4 stored blocks in each half; slots from the count on are ignored.
All inputs are finite; a program needn't handle non-finite values. No bound on the sum of `labels` on one device may be relied on, other than what follows from the above.
Results may differ from a plain program's by a relative error of at most 0.0063.
Values may be sent and summed in bfloat16 or wider, within the bound.
No kernel may reach another device: no remote copies, remote signals or barrier semaphores. Data moves between devices by JAX's collectives and lax.ppermute only.
A program may use at most 64 MiB of HBM per device.

v0:
```python
import jax
import jax.numpy as jnp
from jax import lax
from jax.sharding import PartitionSpec as P

ITERS = 2


def body(blocks, col_index, row_counts, labels, row_weight, feature_scale):
    block_side = blocks.shape[2]
    feat_local = feature_scale.shape[0]
    local_col = col_index - lax.axis_index("feat") * feat_local
    live = (lax.broadcasted_iota(jnp.int32, col_index.shape, 1) < row_counts).astype(jnp.float32)

    def backward(resid):
        rowed = (row_weight * resid).astype(jnp.bfloat16)
        terms = jnp.einsum("rsij,ri->rsj", blocks, rowed, preferred_element_type=jnp.float32)
        terms = terms * live[:, :, None]
        partial_value = jax.ops.segment_sum(
            terms.reshape(-1, block_side), local_col.reshape(-1), num_segments=feat_local
        )
        local_sq = jnp.sum(resid * resid)
        squares = lax.psum(local_sq, "rows")
        total = lax.psum(partial_value, "rows")
        return (total, squares)

    def feat_norm(step_vec):
        local_sq = jnp.sum(step_vec * step_vec)
        squares = lax.psum(local_sq, "feat")
        return jnp.sqrt(squares + 1e-06)

    resid = row_weight * (2 * labels - 1).astype(jnp.float32)
    total, squares = backward(resid)
    beta_now = jnp.sqrt(squares + 1e-06)
    unit_rows = resid / beta_now
    step_vec = feature_scale * total / beta_now
    alpha_now = feat_norm(step_vec)
    unit_feat = step_vec / alpha_now
    phi_bar = beta_now
    rho_bar = alpha_now
    search = unit_feat
    solution = jnp.zeros_like(unit_feat)
    for turn in range(ITERS):
        scaled = (feature_scale * unit_feat).astype(jnp.bfloat16)
        picked = jnp.take(scaled, local_col, axis=0)
        forward_terms = jnp.einsum(
            "rsij,rsj->rsi", blocks, picked, preferred_element_type=jnp.float32
        )
        forward_partial_value = jnp.sum(forward_terms * live[:, :, None], axis=1)
        resid = row_weight * lax.psum(forward_partial_value, "feat") - alpha_now * unit_rows
        total, squares = backward(resid)
        beta_now = jnp.sqrt(squares + 1e-06)
        unit_rows = resid / beta_now
        step_vec = feature_scale * total / beta_now - beta_now * unit_feat
        alpha_now = feat_norm(step_vec)
        unit_feat = step_vec / alpha_now
        rho_now = jnp.sqrt(rho_bar * rho_bar + beta_now * beta_now)
        cosine = rho_bar / rho_now
        sine_part = beta_now / rho_now
        theta_now = sine_part * alpha_now
        rho_bar = -cosine * alpha_now
        phi_now = cosine * phi_bar
        phi_bar = sine_part * phi_bar
        solution = solution + phi_now / rho_now * search
        search = unit_feat - theta_now / rho_now * search
    return (solution, resid)


def solution(mesh):
    return jax.shard_map(
        body,
        mesh=mesh,
        in_specs=(
            P("rows", "feat", None, None),
            P("rows", "feat"),
            P("rows", "feat"),
            P("rows", None),
            P("rows", None),
            P("feat", None),
        ),
        out_specs=(P("feat", None), P("rows", None)),
        check_vma=False,
    )
```

profile of v0, /device:TPU:0, one launch (start us, length us, event | category | flops | bytes accessed | tf_op | source)
XLA Modules:
  0.0 674.8 jit_solution(14838331523554784863)
XLA Ops:
  7.2 0.7 fusion.12
  8.0 0.7 compare_and_fusion
  8.9 1.5 fusion.13
  10.4 8.0 %fusion.10 = f32[128,1,4,128]{3,1,2,0:T(1,128)S(1)} fusion(bf16[128,4,128,128]{3,2,1,0:T(8,128)(2,1)} %param.8, bf16[128,128,1,1]{1,0,2,3:T(8,128)(2,1)S(1)} %get-tuple-element.13), kind=kOutput, calls=%fused_computation.27 | convolution fusion | flops 16777216 | bytes 17072128 | tf_op jit(solution)/shard_map/rsij,ri->rsj/dot_general | solution.py:17
  18.4 0.2 broadcast_multiply_fusion.1
  18.6 3.6 scatter_custom_fusion
  22.4 181.5 %psum.64 = f32[]{:T(128)} all-reduce(f32[]{:T(128)} %get-tuple-element.14), channel_id=1, replica_groups=mesh['rows'=64,'feat'=2] {'rows'}, use_global_device_ids=true, to_apply=%region_3.0 | all-reduce | flops 1 | bytes 8 | tf_op jit(solution)/shard_map/psum | solution.py:23
  204.9 4.0 multiply_reduce_fusion.1
  208.9 3.1 psum.65
  212.7 1.8 multiply_convert_fusion.1
  214.6 1.3 gather_fusion
  215.9 0.2 select_bitcast_fusion.1
  216.1 12.3 %fusion.6 = f32[128,4,1,128]{3,2,1,0:T(1,128)S(1)} fusion(bf16[128,4,128,128]{3,2,1,0:T(8,128)(2,1)} %param.8, bf16[128,4,128,1]{2,1,0,3:T(4,128)(2,1)S(1)} %select_bitcast_fusion.1), kind=kOutput, calls=%fused_computation.17 | convolution fusion | flops 16777216 | bytes 17170432 | tf_op jit(solution)/shard_map/rsij,rsj->rsi/dot_general | solution.py:46
  228.4 0.9 multiply_reduce_fusion.3
  229.3 0.2 all-reduce.9.cloned.1.call-start
  229.5 16.6 %all-reduce.7.cloned.1.call-done = f32[128,128]{1,0:T(8,128)} async-done(((f32[128,128]{1,0:T(8,128)}), f32[128,128]{1,0:T(8,128)}) %all-reduce.7.cloned.1.call-update) | async-done | bytes 65552 | tf_op jit(solution)/shard_map/psum | solution.py:50
  246.1 0.9 fusion.14
  247.0 8.0 %fusion.8 = f32[128,1,4,128]{3,1,2,0:T(1,128)S(1)} fusion(bf16[128,4,128,128]{3,2,1,0:T(8,128)(2,1)} %param.8, bf16[128,128,1,1]{1,0,2,3:T(8,128)(2,1)S(1)} %get-tuple-element.7), kind=kOutput, calls=%fused_computation.25 | convolution fusion | flops 16777216 | bytes 17072128 | tf_op jit(solution)/shard_map/rsij,ri->rsj/dot_general | solution.py:17
  255.3 3.7 scatter_custom_fusion.1
  259.0 0.6 multiply_reduce_fusion.5
  259.6 180.1 %psum.67 = f32[]{:T(128)} all-reduce(f32[]{:T(128)} %multiply_reduce_fusion.5), channel_id=1, replica_groups=mesh['rows'=64,'feat'=2] {'rows'}, use_global_device_ids=true, to_apply=%region_9.11 | all-reduce | flops 1 | bytes 8 | tf_op jit(solution)/shard_map/psum | solution.py:23
  440.4 4.7 multiply_reduce_fusion
  445.1 3.1 psum.69
  448.9 1.8 multiply_convert_fusion
  450.7 1.3 gather_fusion.1
  452.0 0.2 select_bitcast_fusion
  452.3 12.4 %fusion.4 = f32[128,4,1,128]{3,2,1,0:T(1,128)S(1)} fusion(bf16[128,4,128,128]{3,2,1,0:T(8,128)(2,1)} %param.8, bf16[128,4,128,1]{2,1,0,3:T(4,128)(2,1)S(1)} %select_bitcast_fusion), kind=kOutput, calls=%fused_computation.15 | convolution fusion | flops 16777216 | bytes 17170432 | tf_op jit(solution)/shard_map/rsij,rsj->rsi/dot_general | solution.py:46
  464.6 0.9 multiply_reduce_fusion.2
  465.8 16.6 %all-reduce.11.cloned.1.call-done = f32[128,128]{1,0:T(8,128)} async-done(((f32[128,128]{1,0:T(8,128)}), f32[128,128]{1,0:T(8,128)}) %all-reduce.11.cloned.1.call-update) | async-done | bytes 65552 | tf_op jit(solution)/shard_map/psum | solution.py:50
  482.4 2.1 multiply_reduce_fusion.4
  484.5 179.6 %psum.71 = f32[]{:T(128)} all-reduce(f32[]{:T(128)} %get-tuple-element.3), channel_id=1, replica_groups=mesh['rows'=64,'feat'=2] {'rows'}, use_global_device_ids=true, to_apply=%region_17.19 | all-reduce | flops 1 | bytes 8 | tf_op jit(solution)/shard_map/psum | solution.py:23
  664.9 3.4 multiply_add_fusion
  (25 shorter events, 1.0 us)
Async XLA Ops:
  7.2 197.8 %all-reduce.5.cloned.1.call-start = ((), (), s32[]{:S(2)}) async-start(), calls=%async_computation | async-start | bytes 4194304 | tf_op jit(solution)/shard_map/psum | solution.py:24
  18.6 186.3 %copy-start = (f32[4096,128]{1,0:T(8,128)S(1)}, f32[4096,128]{1,0:T(8,128)}, u32[]{:S(2)}) copy-start(f32[4096,128]{1,0:T(8,128)} %param.13) | copy-start | bytes 6291460
  22.3 223.8 %all-reduce.7.cloned.1.call-start = ((), (), s32[]{:S(2)}) async-start(), calls=%async_computation.1 | async-start | bytes 131072 | tf_op jit(solution)/shard_map/psum | solution.py:50
  216.1 30.0 %copy-start.2 = (f32[128,128]{1,0:T(8,128)S(1)}, f32[128,128]{1,0:T(8,128)}, u32[]{:S(2)}) copy-start(f32[128,128]{1,0:T(8,128)} %param.12) | copy-start | bytes 196612
  216.1 30.0 %copy-start.3 = (s32[128,128]{1,0:T(8,128)S(1)}, s32[128,128]{1,0:T(8,128)}, u32[]{:S(2)}) copy-start(s32[128,128]{1,0:T(8,128)} %param.11) | copy-start | bytes 196612
  229.3 211.1 %all-reduce.9.cloned.1.call-start = ((), (), s32[]{:S(2)}) async-start(), calls=%async_computation.2 | async-start | bytes 4194304 | tf_op jit(solution)/shard_map/psum | solution.py:24
  259.0 223.4 %all-reduce.11.cloned.1.call-start = ((), (), s32[]{:S(2)}) async-start(), calls=%async_computation.3 | async-start | bytes 131072 | tf_op jit(solution)/shard_map/psum | solution.py:50
  452.3 212.6 %copy-start.1 = (f32[4096,128]{1,0:T(8,128)S(1)}, f32[4096,128]{1,0:T(8,128)}, u32[]{:S(2)}) copy-start(f32[4096,128]{1,0:T(8,128)} %get-tuple-element.12) | copy-start | bytes 6291460
Sparse Core Ops, SparseCore 0:
  22.4 135.0 all-reduce.4
  229.4 16.6 all-reduce.6
  259.1 133.9 all-reduce.8
  465.7 16.6 all-reduce.10
where the time goes:
time: 675 us
  blocking collectives  547 us (81%)
  matrix products  40.7 us (6%)
  waiting for transfers between devices  33.3 us (5%)
  other arithmetic  32.2 us (5%)
  between operations  17.7 us (3%)
    psum x3, blocking collectives, backward(): squares = lax.psum(local_sq, 'rows')  541 us
    psum x2, waiting for transfers between devices, body(): lax.psum(forward_partial_value, 'feat')  33.2 us
    dot_general x2, matrix products, body(): jnp.einsum('rsij,rsj->rsi', blocks, picked, preferred_element_type=jnp.fl...  24.6 us
    dot_general x2, matrix products, backward(): jnp.einsum('rsij,ri->rsj', blocks, rowed, preferred_element_type=jnp.floa...  16.1 us
  transfers between devices with their start and end apart: 4, of which 2 were waited for; matrix products, arithmetic and copies ran while one was open for 0% of the time, Pallas kernels for 0%

commit v1 on v0

--- a/solution.py
+++ b/solution.py
@@ -47,7 +47,10 @@
             "rsij,rsj->rsi", blocks, picked, preferred_element_type=jnp.float32
         )
         forward_partial_value = jnp.sum(forward_terms * live[:, :, None], axis=1)
-        resid = row_weight * lax.psum(forward_partial_value, "feat") - alpha_now * unit_rows
+        resid = (
+            row_weight * jnp.sum(lax.all_gather(forward_partial_value, "feat"), axis=0)
+            - alpha_now * unit_rows
+        )
         total, squares = backward(resid)
         beta_now = jnp.sqrt(squares + 1e-06)
         unit_rows = resid / beta_now

time: 675 us -> 630 us (0.933)
  waiting for transfers between devices: 33.3 us -> 0.08 us
  blocking collectives: 547 us -> 538 us
    psum x2 -> x0, waiting for transfers between devices: 33.2 us -> none  [body(): lax.psum(forward_partial_value, 'feat')]
    psum x3, blocking collectives: 541 us -> 528 us  [backward(): squares = lax.psum(local_sq, 'rows')]
  transfers between devices with their start and end apart: 4 -> 2, of which waited for: 2 -> 0; matrix products, arithmetic and copies ran while one was open for 0% -> 0% of each run, Pallas kernels for 0% -> 0%
where the time goes in v1:
time: 630 us
  blocking collectives  538 us (85%)
  matrix products  40.7 us (6%)
  other arithmetic  29.2 us (5%)
  between operations  18 us (3%)
    psum x3, blocking collectives, backward(): squares = lax.psum(local_sq, 'rows')  528 us
    dot_general x2, matrix products, body(): jnp.einsum('rsij,rsj->rsi', blocks, picked, preferred_element_type=jnp.fl...  24.7 us
    dot_general x2, matrix products, backward(): jnp.einsum('rsij,ri->rsj', blocks, rowed, preferred_element_type=jnp.floa...  16.1 us
  transfers between devices with their start and end apart: 2, of which 0 were waited for; matrix products, arithmetic and copies ran while one was open for 0% of the time, Pallas kernels for 0%

profile of v1, /device:TPU:0, one launch (start us, length us, event | category | flops | bytes accessed | tf_op | source)
XLA Modules:
  0.0 629.8 jit_solution(15332653727602939242)
XLA Ops:
  7.2 0.7 fusion.12
  8.0 0.7 compare_and_fusion
  8.9 1.5 fusion.13
  10.4 8.0 %fusion.10 = f32[128,1,4,128]{3,1,2,0:T(1,128)S(1)} fusion(bf16[128,4,128,128]{3,2,1,0:T(8,128)(2,1)} %param.8, bf16[128,128,1,1]{1,0,2,3:T(8,128)(2,1)S(1)} %get-tuple-element.13), kind=kOutput, calls=%fused_computation.27 | convolution fusion | flops 16777216 | bytes 17072128 | tf_op jit(solution)/shard_map/rsij,ri->rsj/dot_general | solution.py:17
  18.4 0.2 broadcast_multiply_fusion.1
  18.6 3.6 scatter_custom_fusion
  22.4 181.5 %psum.50 = f32[]{:T(128)} all-reduce(f32[]{:T(128)} %get-tuple-element.14), channel_id=1, replica_groups=mesh['rows'=64,'feat'=2] {'rows'}, use_global_device_ids=true, to_apply=%region_3.0 | all-reduce | flops 1 | bytes 8 | tf_op jit(solution)/shard_map/psum | solution.py:23
  204.8 0.1 copy.16
  204.9 4.0 multiply_reduce_fusion.1
  208.9 3.1 psum.51
  212.7 1.8 multiply_convert_fusion.1
  214.6 1.3 gather_fusion
  215.9 0.2 select_bitcast_fusion.1
  216.1 12.3 %fusion.6 = f32[128,4,1,128]{3,2,1,0:T(1,128)S(1)} fusion(bf16[128,4,128,128]{3,2,1,0:T(8,128)(2,1)} %param.8, bf16[128,4,128,1]{2,1,0,3:T(4,128)(2,1)S(1)} %select_bitcast_fusion.1), kind=kOutput, calls=%fused_computation.17 | convolution fusion | flops 16777216 | bytes 17170432 | tf_op jit(solution)/shard_map/rsij,rsj->rsi/dot_general | solution.py:46
  228.4 0.2 multiply_reduce_fusion.3
  228.7 2.1 all-gather
  230.8 8.0 %fusion.8 = f32[128,1,4,128]{3,1,2,0:T(1,128)S(1)} fusion(bf16[128,4,128,128]{3,2,1,0:T(8,128)(2,1)} %param.8, bf16[128,128,1,1]{1,0,2,3:T(8,128)(2,1)S(1)} %get-tuple-element.7), kind=kOutput, calls=%fused_computation.25 | convolution fusion | flops 16777216 | bytes 17072128 | tf_op jit(solution)/shard_map/rsij,ri->rsj/dot_general | solution.py:17
  238.9 0.2 broadcast_multiply_fusion
  239.1 3.7 scatter_custom_fusion.1
  242.8 0.6 multiply_reduce_fusion.5
  243.4 172.8 %psum.52 = f32[]{:T(128)} all-reduce(f32[]{:T(128)} %multiply_reduce_fusion.5), channel_id=1, replica_groups=mesh['rows'=64,'feat'=2] {'rows'}, use_global_device_ids=true, to_apply=%region_9.11 | all-reduce | flops 1 | bytes 8 | tf_op jit(solution)/shard_map/psum | solution.py:23
  417.1 4.7 multiply_reduce_fusion
  421.7 3.1 psum.54
  425.5 1.8 multiply_convert_fusion
  427.3 1.3 gather_fusion.1
  428.7 0.2 select_bitcast_fusion
  428.9 12.4 %fusion.4 = f32[128,4,1,128]{3,2,1,0:T(1,128)S(1)} fusion(bf16[128,4,128,128]{3,2,1,0:T(8,128)(2,1)} %param.8, bf16[128,4,128,1]{2,1,0,3:T(4,128)(2,1)S(1)} %select_bitcast_fusion), kind=kOutput, calls=%fused_computation.15 | convolution fusion | flops 16777216 | bytes 17170432 | tf_op jit(solution)/shard_map/rsij,rsj->rsi/dot_general | solution.py:46
  441.3 0.3 multiply_reduce_fusion.2
  441.5 1.9 all-gather.1
  443.4 1.3 multiply_reduce_fusion.4
  444.7 174.0 %psum.55 = f32[]{:T(128)} all-reduce(f32[]{:T(128)} %get-tuple-element.3), channel_id=1, replica_groups=mesh['rows'=64,'feat'=2] {'rows'}, use_global_device_ids=true, to_apply=%region_17.19 | all-reduce | flops 1 | bytes 8 | tf_op jit(solution)/shard_map/psum | solution.py:23
  619.6 3.4 multiply_add_fusion
  (23 shorter events, 0.7 us)
Async XLA Ops:
  7.2 197.8 %all-reduce.3.cloned.1.call-start = ((), (), s32[]{:S(2)}) async-start(), calls=%async_computation | async-start | bytes 4194304 | tf_op jit(solution)/shard_map/psum | solution.py:24
  18.6 186.3 %copy-start = (f32[4096,128]{1,0:T(8,128)S(1)}, f32[4096,128]{1,0:T(8,128)}, u32[]{:S(2)}) copy-start(f32[4096,128]{1,0:T(8,128)} %param.13) | copy-start | bytes 6291460
  22.3 394.7 %all-reduce.5.cloned.1.call-start = ((), (), s32[]{:S(2)}) async-start(), calls=%async_computation.1 | async-start | bytes 4194304 | tf_op jit(solution)/shard_map/psum | solution.py:24
  216.1 14.6 %copy-start.2 = (f32[128,128]{1,0:T(8,128)S(1)}, f32[128,128]{1,0:T(8,128)}, u32[]{:S(2)}) copy-start(f32[128,128]{1,0:T(8,128)} %param.12) | copy-start | bytes 196612
  216.1 14.6 %copy-start.3 = (s32[128,128]{1,0:T(8,128)S(1)}, s32[128,128]{1,0:T(8,128)}, u32[]{:S(2)}) copy-start(s32[128,128]{1,0:T(8,128)} %param.11) | copy-start | bytes 196612
  428.9 190.7 %copy-start.1 = (f32[4096,128]{1,0:T(8,128)S(1)}, f32[4096,128]{1,0:T(8,128)}, u32[]{:S(2)}) copy-start(f32[4096,128]{1,0:T(8,128)} %get-tuple-element.12) | copy-start | bytes 6291460
Sparse Core Ops, SparseCore 0:
  22.4 135.0 all-reduce.2
  242.9 126.0 all-reduce.4
